TPU v7x, 32 devices: a whole 2x2x4 slice. The times are simulated.
32 devices in a mesh: shot: 2 (over y), row: 4 (over x, core), freq: 4 (over z).
Axes of the slice: x: 2, y: 2, z: 4, core: 2. Of those that a mesh axis runs over, the one named last changes fastest.
Arguments:
- source_field: float32 [2, 8, 1024, 1024], P(None, ('shot', 'freq'), 'row'), parts along dimension 1, may hold values from -6 to 6
- receiver_field: float32 [2, 8, 1024, 1024], P(None, ('shot', 'freq'), 'row'), parts along dimension 1, may hold values from -6 to 6
- slowness: float32 [4, 1024, 1024], P('freq', 'row'), may hold values from 0.22 to 0.67
- owner: int32 [4], replicated, may hold values from 0 to 3, each once
- freq_index: int32 [8], P(('shot', 'freq')), parts along dimension 0, may hold values from 0 to 3, each once
Outputs:
- source_out: float32 [2, 8, 1024, 1024], P(None, ('shot', 'freq'), 'row'), parts along dimension 1
- receiver_out: float32 [2, 8, 1024, 1024], P(None, ('shot', 'freq'), 'row'), parts along dimension 1
- image: float32 [4, 1024, 1024], P('shot', 'row', 'freq'), parts along dimension 0
There are 2 independent parts, one for each index of `shot`. A program takes and returns all parts, laid end to end along the dimension named above; an argument that names none is the same for every part. Nothing has to cross between parts.
All inputs are finite; a program needn't handle non-finite values.
Results may differ from a plain program's by a relative error of at most 0.00022.
Values sent between devices are 32-bit elements; how exact they have to be, the bound alone decides.
A program may use at most 128 MiB of HBM per device.

v0:
```python
import math
import jax
import jax.numpy as jnp
from jax import lax
from jax.sharding import PartitionSpec as P

NZ = 2
dz_km = 0.01
dx_km = 0.0125
ref_slow = 0.5
base_hertz = 3.0
step_hertz = 4.0
taper = 0.5


def spread(value, axis, source):
    kept = jnp.where(lax.axis_index(axis) == source, value, 0).astype(value.dtype)
    return lax.psum(kept, axis)


def split_length(length):
    return length // 128


def angle_table(count_a, count_b, modulus, sign):
    left = jnp.arange(count_a, dtype=jnp.int32)[:, None]
    right = jnp.arange(count_b, dtype=jnp.int32)[None, :]
    turns = (left * right % modulus).astype(jnp.float32) * (2.0 * math.pi / modulus)
    return (jnp.cos(turns), sign * jnp.sin(turns))


def contract(form, left, right):
    return jnp.einsum(form, left, right, precision=lax.Precision.HIGHEST)


def transform_pair(real_part, imag_part, sign, last):
    length = real_part.shape[2] if last else real_part.shape[1]
    first = split_length(length)
    second = length // first
    cos_a, sin_a = angle_table(first, first, first, sign)
    cos_b, sin_b = angle_table(second, second, second, sign)
    twist_c, twist_s = angle_table(first, second, length, sign)
    if last:
        shape = (real_part.shape[0], real_part.shape[1], first, second)
        form_one = "fajb,jk->fakb"
        form_two = "fakb,bm->famk"
    else:
        shape = (real_part.shape[0], first, second, real_part.shape[2])
        form_one = "fjbq,jk->fkbq"
        form_two = "fkbq,bm->fmkq"
        twist_c = twist_c[:, :, None]
        twist_s = twist_s[:, :, None]
    x_re = real_part.reshape(shape)
    x_im = imag_part.reshape(shape)
    y_re = contract(form_one, x_re, cos_a) - contract(form_one, x_im, sin_a)
    y_im = contract(form_one, x_im, cos_a) + contract(form_one, x_re, sin_a)
    z_re = y_re * twist_c - y_im * twist_s
    z_im = y_im * twist_c + y_re * twist_s
    out_re = contract(form_two, z_re, cos_b) - contract(form_two, z_im, sin_b)
    out_im = contract(form_two, z_im, cos_b) + contract(form_two, z_re, sin_b)
    return (out_re.reshape(real_part.shape), out_im.reshape(real_part.shape))


def transform(block, sign, last):
    count = block.shape[0]
    freqs = block.shape[2]
    plane = block.shape[3:]
    real_part = block[:, 0].reshape((count * freqs,) + plane)
    imag_part = block[:, 1].reshape((count * freqs,) + plane)
    out_re, out_im = transform_pair(real_part, imag_part, sign, last)
    shape = (count, freqs) + plane
    return jnp.stack([out_re.reshape(shape), out_im.reshape(shape)], axis=1)


def wavenumbers(length, start, count):
    index = start + jnp.arange(count, dtype=jnp.int32)
    signed = jnp.where(index * 2 < length, index, index - length)
    return signed.astype(jnp.float32) * (2.0 * math.pi / (length * dx_km))


def rotate(block, cos_v, sin_v):
    real_part = block[:, 0]
    imag_part = block[:, 1]
    return jnp.stack(
        [real_part * cos_v - imag_part * sin_v, imag_part * cos_v + real_part * sin_v], axis=1
    )


def shift_phase(block, omega, kx_part, ky_part, total):
    square = kx_part[:, None] ** 2 + ky_part[None, :] ** 2
    kmax = math.pi / dx_km
    damp = jnp.exp(-taper * square / (kmax * kmax)) / total
    ws0 = omega[:, None, None] * ref_slow
    vertical = ws0 - 0.5 * square[None] / ws0
    cos_v = jnp.cos(dz_km * vertical) * damp
    sin_v = jnp.sin(dz_km * vertical) * damp
    return rotate(block, cos_v, sin_v)


def correct(block, slab, omega):
    theta = omega[:, None, None] * (slab[None] - ref_slow) * dz_km
    return rotate(block, jnp.cos(theta), jnp.sin(theta))


def image_term(block):
    return jnp.sum(block[0, 0] * block[1, 0] - block[0, 1] * block[1, 1], axis=0)


def body(source_field, receiver_field, slowness, owner, freq_index):
    rows = source_field.shape[2]
    width = source_field.shape[3]
    row_count = lax.axis_size("row")
    height = rows * row_count
    cols = width // row_count
    place = lax.axis_index("row")
    omega = 2.0 * math.pi * (base_hertz + step_hertz * freq_index.astype(jnp.float32))
    mirrored = jnp.stack([receiver_field[0], -receiver_field[1]])
    fields = jnp.stack([source_field, mirrored])
    kx_all = wavenumbers(height, 0, height)
    ky_own = wavenumbers(width, place * cols, cols)
    total = float(height * width)
    slab_dev = slowness.shape[0]
    images = []
    for depth in range(NZ):
        chosen = owner[depth]
        held = spread(slowness, "freq", chosen // slab_dev)
        slab = lax.dynamic_index_in_dim(held, chosen % slab_dev, 0, keepdims=False)
        fields = transform(fields, -1.0, True)
        fields = lax.all_to_all(fields, "row", split_axis=4, concat_axis=3, tiled=True)
        items = fields
        items = transform(items, -1.0, False)
        items = shift_phase(items, omega, kx_all, ky_own, total)
        fields = transform(items, 1.0, False)
        fields = lax.all_to_all(fields, "row", split_axis=3, concat_axis=4, tiled=True)
        fields = transform(fields, 1.0, True)
        fields = correct(fields, slab, omega)
        images.append(image_term(fields))
    parts = [lax.psum_scatter(term, "freq", scatter_dimension=1, tiled=True) for term in images]
    image = jnp.stack(parts)
    source_out = fields[0]
    receiver_out = jnp.stack([fields[1, 0], -fields[1, 1]])
    return (source_out, receiver_out, image)


def solution(mesh):
    in_specs = (
        P(None, ("shot", "freq"), "row", None),
        P(None, ("shot", "freq"), "row", None),
        P("freq", "row", None),
        P(),
        P(("shot", "freq")),
    )
    out_specs = (
        P(None, ("shot", "freq"), "row", None),
        P(None, ("shot", "freq"), "row", None),
        P("shot", "row", "freq"),
    )
    return jax.shard_map(body, mesh=mesh, in_specs=in_specs, out_specs=out_specs, check_vma=False)
```

profile of v0, /device:TPU:0, one launch (start us, length us, event | category | flops | bytes accessed | tf_op | source)
XLA Modules:
  0.0 596.2 jit_solution(643073891319918496)
XLA Ops:
  32.7 5.4 copy.346
  38.1 4.9 all-to-all-start
  44.0 4.0 fusion.186
  48.1 43.7 %all-to-all-done = f32[2,2,1,256,1024]{3,0,2,1,4:T(2,128)} async-done(((f32[2,2,1,256,1024]{3,0,2,1,4:T(2,128)}), f32[2,2,1,256,1024]{3,0,2,1,4:T(2,128)}, u32[]{:S(2)}, u32[]{:S(2)}) %all-to-all-start) | async-done | bytes 4194336 | tf_op jit(solution)/shard_map/all_to_all | solution.py:129
  91.8 5.0 copy.347
  96.7 5.4 copy.348
  113.4 3.8 subtract_bitcast_fusion.13
  139.8 3.9 subtract_bitcast_fusion.11
  157.1 5.2 copy.372
  162.4 5.0 all-to-all-start.1
  171.0 90.0 %all-reduce.3.cloned.1.call-done = (f32[1,256,1024]{2,1,0:T(8,128)}, f32[1,256,1024]{2,1,0:T(8,128)}) async-done(((f32[1,256,1024]{2,1,0:T(8,128)}, f32[1,256,1024]{2,1,0:T(8,128)}), (f32[1,256,1024]{2,1,0:T(8,128)}, f32[1,256,1024]{2,1,0:T(8,128)})) %all-reduce.3.cloned.1.call-update) | async-done | bytes 2097168 | tf_op jit(solution)/shard_map/psum | solution.py:18
  260.9 4.7 fusion.192
  268.6 5.0 copy.373
  273.6 5.3 copy.374
  278.9 4.6 fusion.663
  315.4 4.8 fusion.314
  323.3 3.6 fusion.316
  343.5 3.2 copy.395
  346.8 50.7 %all_to_all.72 = f32[2,2,1,256,1024]{3,0,2,1,4:T(2,128)S(1)} all-to-all(f32[2,2,1,256,1024]{3,0,2,1,4:T(2,128)S(1)} %copy.395), channel_id=1, replica_groups=mesh['shot'=2,'row'=4,'freq'=4] {'row'}, dimensions={4} | all-to-all | bytes 8388608 | tf_op jit(solution)/shard_map/all_to_all | solution.py:129
  400.3 5.7 copy.397
  417.2 3.6 subtract_bitcast_fusion.5
  443.4 4.0 subtract_bitcast_fusion.3
  460.8 5.2 copy.418
  466.0 4.9 all-to-all-start.3
  474.9 5.7 cosine_bitcast_fusion
  484.7 4.7 fusion.10
  490.7 28.5 %all-to-all-done.3 = f32[2,2,1,1024,256]{4,0,2,1,3:T(2,128)} async-done(((f32[2,2,1,1024,256]{4,0,2,1,3:T(2,128)}), f32[2,2,1,1024,256]{4,0,2,1,3:T(2,128)}, u32[]{:S(2)}, u32[]{:S(2)}) %all-to-all-start.3) | async-done | bytes 4194336 | tf_op jit(solution)/shard_map/all_to_all | solution.py:134
  519.2 5.0 copy.419
  524.2 5.3 copy.420
  529.4 4.6 fusion.661
  568.1 4.3 fusion.14
  574.3 13.1 %reduce-scatter.5.cloned.1.call-done = f32[256,256]{0,1:T(8,128)} async-done(((f32[256,1024]{0,1:T(8,128)}), f32[256,256]{0,1:T(8,128)}) %reduce-scatter.5.cloned.1.call-update) | async-done | bytes 262160 | tf_op jit(solution)/shard_map/reduce_scatter | solution.py:138
  (169 shorter events, 226.1 us)
Async XLA Ops:
  8.9 1.6 copy-start.19
  38.1 53.7 %all-to-all-start = ((f32[2,2,1,256,1024]{3,0,2,1,4:T(2,128)}), f32[2,2,1,256,1024]{3,0,2,1,4:T(2,128)}, u32[]{:S(2)}, u32[]{:S(2)}) async-start(f32[2,2,1,256,1024]{3,0,2,1,4:T(2,128)} %copy.346), calls=%async_computation | async-start | bytes 8388608 | tf_op jit(solution)/shard_map/all_to_all | solution.py:129
  48.1 82.2 %copy-start.8 = (f32[8,128,256]{2,1,0:T(8,128)}, f32[8,128,256]{2,1,0:T(8,128)S(1)}, u32[]{:S(2)}) copy-start(f32[8,128,256]{2,1,0:T(8,128)S(1)} %get-tuple-element.67) | copy-start | bytes 3145732
  162.4 5.1 copy-start.21
  162.4 7.0 %copy-start.20 = (f32[1,256,1024]{2,1,0:T(8,128)S(1)}, f32[1,256,1024]{2,1,0:T(8,128)}, u32[]{:S(2)}) copy-start(f32[1,256,1024]{2,1,0:T(8,128)} %param.7) | copy-start | bytes 3145732
  162.4 106.2 %all-to-all-start.1 = ((f32[2,2,1,1024,256]{4,0,2,1,3:T(2,128)}), f32[2,2,1,1024,256]{4,0,2,1,3:T(2,128)}, u32[]{:S(2)}, u32[]{:S(2)}) async-start(f32[2,2,1,1024,256]{4,0,2,1,3:T(2,128)} %copy.372), calls=%async_computation.1 | async-start | bytes 8388608 | tf_op jit(solution)/shard_map/all_to_all | solution.py:134
  167.4 93.5 %all-reduce.3.cloned.1.call-start = ((), (), s32[]{:S(2)}) async-start(), calls=%async_computation.8 | async-start | bytes 4194304 | tf_op jit(solution)/shard_map/psum | solution.py:18
  265.7 2.9 copy-start.11
  265.7 2.9 copy-start.13
  285.6 3.2 copy-start.6
  291.1 1.9 copy-start.14
  293.0 2.0 copy-start.7
  307.1 1.3 copy-start.1
  308.4 1.2 copy-start.17
  308.4 1.5 copy-start.18
  323.2 3.6 copy-start.2
  323.3 3.6 copy-start.15
  326.9 2.0 copy-start.5
  432.6 1.2 copy-start.9
  466.0 53.1 %all-to-all-start.3 = ((f32[2,2,1,1024,256]{4,0,2,1,3:T(2,128)}), f32[2,2,1,1024,256]{4,0,2,1,3:T(2,128)}, u32[]{:S(2)}, u32[]{:S(2)}) async-start(f32[2,2,1,1024,256]{4,0,2,1,3:T(2,128)} %copy.418), calls=%async_computation.3 | async-start | bytes 8388608 | tf_op jit(solution)/shard_map/all_to_all | solution.py:134
  470.9 2.7 copy-start.12
  470.9 103.4 %reduce-scatter.3.cloned.1.call-start = ((), (), s32[]{:S(2)}) async-start(), calls=%async_computation.6 | async-start | bytes 1310720 | tf_op jit(solution)/shard_map/reduce_scatter | solution.py:138
  490.7 96.8 %reduce-scatter.5.cloned.1.call-start = ((), (), s32[]{:S(2)}) async-start(), calls=%async_computation.7 | async-start | bytes 1310720 | tf_op jit(solution)/shard_map/reduce_scatter | solution.py:138
  536.1 3.2 copy-start.3
  541.8 1.9 copy-start.16
  543.7 2.0 copy-start.4
  555.2 2.3 copy-start.10
  557.5 2.5 copy-start
Sparse Core Ops, SparseCore 0:
  171.2 89.6 all-reduce.2
  490.8 26.5 reduce-scatter.2
  562.2 25.1 reduce-scatter.4
where the time goes:
time: 606 us; the launch traced here: 596 us
  waiting for transfers between devices  175 us (29%)
  matrix products  170 us (28%)
  local copies, waits for them, and re-layouts  125 us (21%)
  blocking collectives  50.7 us (8%)
  other arithmetic  42.9 us (7%)
  between operations  17.4 us (3%)
  starting transfers between devices  14.9 us (2%)
    dot_general x64, matrix products, contract(): return jnp.einsum(form, left, right, precision=lax.Precision.HIGHEST)  170 us
    psum x1, waiting for transfers between devices, spread(): return lax.psum(kept, axis)  90 us
    all_to_all x1, blocking collectives, body(): lax.all_to_all(fields, 'row', split_axis=4, concat_axis=3, tiled=True)  50.7 us
    all_to_all x1, waiting for transfers between devices, body(): lax.all_to_all(fields, 'row', split_axis=4, concat_axis=3, tiled=True)  43.7 us
    all_to_all x2, waiting for transfers between devices, body(): lax.all_to_all(fields, 'row', split_axis=3, concat_axis=4, tiled=True)  28.5 us
    all_to_all x4, local copies, waits for them, and re-layouts, body(): lax.all_to_all(fields, 'row', split_axis=3, concat_axis=4, tiled=True)  20.5 us
    another operation x4, local copies, waits for them, and re-layouts, transform(): return jnp.stack([out_re.reshape(shape), out_im.reshape(shape)], axis=1)  19.1 us
    all_to_all x4, local copies, waits for them, and re-layouts, body(): lax.all_to_all(fields, 'row', split_axis=4, concat_axis=3, tiled=True)  18.9 us
  transfers between devices with their start and end apart: 6, of which 4 were waited for; matrix products, arithmetic and copies ran while one was open for 15% of the time, Pallas kernels for 0%

commit v1 on v0

--- a/solution.py
+++ b/solution.py
@@ -11,6 +11,18 @@
 base_hertz = 3.0
 step_hertz = 4.0
 taper = 0.5
+
+
+def in_blocks(x, dim, peers):
+    shape = x.shape
+    tiles = x.reshape(*shape[:dim], peers, shape[dim] // peers, *shape[dim + 1 :])
+    return jnp.moveaxis(tiles, dim, 0)
+
+
+def joined_along(blocks, dim):
+    blocks = jnp.moveaxis(blocks, 0, dim)
+    lengths = blocks.shape
+    return blocks.reshape(*lengths[:dim], lengths[dim] * lengths[dim + 1], *lengths[dim + 2 :])
 
 
 def spread(value, axis, source):
@@ -131,7 +143,14 @@
         items = transform(items, -1.0, False)
         items = shift_phase(items, omega, kx_all, ky_own, total)
         fields = transform(items, 1.0, False)
-        fields = lax.all_to_all(fields, "row", split_axis=3, concat_axis=4, tiled=True)
+        peers, index_2 = (lax.axis_size("row"), lax.axis_index("row"))
+        blocks = in_blocks(fields, 3, peers)
+        done = [blocks[index_2]]
+        for step in range(1, peers):
+            sent = blocks[(index_2 + step) % peers]
+            done.append(lax.ppermute(sent, "row", [(i, (i + step) % peers) for i in range(peers)]))
+        blocks = jnp.stack(done)[(index_2 - jnp.arange(peers)) % peers]
+        fields = joined_along(blocks, 4)
         fields = transform(fields, 1.0, True)
         fields = correct(fields, slab, omega)
         images.append(image_term(fields))

time: 606 us -> 553 us (0.913)
  blocking collectives: 50.7 us -> 0 us
  waiting for transfers between devices: 175 us -> 162 us
  other arithmetic: 42.9 us -> 52.3 us
    psum x1, waiting for transfers between devices: 90 us -> 0.02 us  [spread(): return lax.psum(kept, axis)]
    ppermute x0 -> x6, waiting for transfers between devices: none -> 59.3 us  [body(): lax.ppermute(sent, 'row', [(i, (i + step) % peers) for i in range(peers)])]
    all_to_all x1 -> x0, blocking collectives: 50.7 us -> none  [body(): lax.all_to_all(fields, 'row', split_axis=4, concat_axis=3, tiled=True)]
    all_to_all x1 -> x2, waiting for transfers between devices: 43.7 us -> 83.3 us  [body(): lax.all_to_all(fields, 'row', split_axis=4, concat_axis=3, tiled=True)]
    all_to_all x2 -> x0, waiting for transfers between devices: 28.5 us -> none  [body(): lax.all_to_all(fields, 'row', split_axis=3, concat_axis=4, tiled=True)]
    all_to_all x4 -> x0, local copies, waits for them, and re-layouts: 20.5 us -> none  [body(): lax.all_to_all(fields, 'row', split_axis=3, concat_axis=4, tiled=True)]
    transpose x0 -> x2, local copies, waits for them, and re-layouts: none -> 10.5 us  [joined_along(): blocks = jnp.moveaxis(blocks, 0, dim)]
    gather x0 -> x2, local copies, waits for them, and re-layouts: none -> 10 us  [body(): blocks = jnp.stack(done)[(index_2 - jnp.arange(peers)) % peers]]
  transfers between devices with their start and end apart: 6 -> 11, of which waited for: 4 -> 9; matrix products, arithmetic and copies ran while one was open for 15% -> 31% of each run, Pallas kernels for 0% -> 0%
where the time goes in v1:
time: 553 us; the launch traced here: 543 us
  matrix products  170 us (31%)
  waiting for transfers between devices  162 us (29%)
  local copies, waits for them, and re-layouts  128 us (23%)
  other arithmetic  52.3 us (9%)
  between operations  17.4 us (3%)
  starting transfers between devices  13.5 us (2%)
    dot_general x64, matrix products, contract(): return jnp.einsum(form, left, right, precision=lax.Precision.HIGHEST)  170 us
    all_to_all x2, waiting for transfers between devices, body(): lax.all_to_all(fields, 'row', split_axis=4, concat_axis=3, tiled=True)  83.3 us
    ppermute x6, waiting for transfers between devices, body(): lax.ppermute(sent, 'row', [(i, (i + step) % peers) for i in range(peers)])  59.3 us
    all_to_all x4, local copies, waits for them, and re-layouts, body(): lax.all_to_all(fields, 'row', split_axis=4, concat_axis=3, tiled=True)  21 us
    reduce_scatter x2, waiting for transfers between devices, body(): lax.psum_scatter(term, 'freq', scatter_dimension=1, tiled=True)  19.2 us
    sub x5, other arithmetic, rotate(): real_part * cos_v - imag_part * sin_v  12.8 us
  transfers between devices with their start and end apart: 11, of which 9 were waited for; matrix products, arithmetic and copies ran while one was open for 31% of the time, Pallas kernels for 0%

profile of v1, /device:TPU:0, one launch (start us, length us, event | category | flops | bytes accessed | tf_op | source)
XLA Modules:
  0.0 542.8 jit_solution(14480310383921981788)
XLA Ops:
  32.7 5.4 copy.362
  38.1 5.0 all-to-all-start
  47.7 4.0 fusion.186
  51.8 40.1 %all-to-all-done = f32[2,2,1,256,1024]{3,0,2,1,4:T(2,128)} async-done(((f32[2,2,1,256,1024]{3,0,2,1,4:T(2,128)}), f32[2,2,1,256,1024]{3,0,2,1,4:T(2,128)}, u32[]{:S(2)}, u32[]{:S(2)}) %all-to-all-start) | async-done | bytes 4194336 | tf_op jit(solution)/shard_map/all_to_all | solution.py:141
  91.9 5.0 copy.363
  96.9 5.6 %copy.364 = f32[2,2,1,4,256,256]{5,4,3,1,0,2:T(8,128)} copy(f32[2,2,1,4,256,256]{4,5,3,1,0,2:T(8,128)} %bitcast.484) | data formatting | bytes 8388608 | tf_op jit(solution)/shard_map/all_to_all | solution.py:141
  113.7 3.8 subtract_bitcast_fusion.13
  140.1 3.7 subtract_bitcast_fusion.11
  163.5 4.7 fusion.200
  172.5 11.1 %collective-permute-done = f32[2,2,1,256,256]{4,3,1,0,2:T(8,128)} collective-permute-done((f32[2,2,1,256,256]{4,3,1,0,2:T(8,128)}, f32[2,2,1,256,256]{4,3,1,0,2:T(8,128)}, u32[]{:S(2)}, u32[]{:S(2)}) %collective-permute-start) | collective-permute-done | bytes 1048608 | tf_op jit(solution)/shard_map/ppermute | solution.py:151
  187.1 18.1 %collective-permute-done.2 = f32[2,2,1,256,256]{4,3,1,0,2:T(8,128)} collective-permute-done((f32[2,2,1,256,256]{4,3,1,0,2:T(8,128)}, f32[2,2,1,256,256]{4,3,1,0,2:T(8,128)}, u32[]{:S(2)}, u32[]{:S(2)}) %collective-permute-start.2) | collective-permute-done | bytes 1048608 | tf_op jit(solution)/shard_map/ppermute | solution.py:151
  205.2 4.2 maximum_bitcast_fusion
  209.4 5.0 gather_fusion
  214.4 5.3 copy.392
  219.7 4.6 fusion.641
  256.0 4.8 fusion.322
  284.4 5.2 copy.413
  289.6 4.9 all-to-all-start.1
  299.7 43.1 %all-to-all-done.1 = f32[2,2,1,256,1024]{3,0,2,1,4:T(2,128)} async-done(((f32[2,2,1,256,1024]{3,0,2,1,4:T(2,128)}), f32[2,2,1,256,1024]{3,0,2,1,4:T(2,128)}, u32[]{:S(2)}, u32[]{:S(2)}) %all-to-all-start.1) | async-done | bytes 4194336 | tf_op jit(solution)/shard_map/all_to_all | solution.py:141
  342.8 5.0 copy.414
  347.8 5.4 %copy.415 = f32[2,2,1,4,256,256]{5,4,3,1,0,2:T(8,128)} copy(f32[2,2,1,4,256,256]{4,5,3,1,0,2:T(8,128)} %bitcast.486) | data formatting | bytes 8388608 | tf_op jit(solution)/shard_map/all_to_all | solution.py:141
  364.5 3.8 subtract_bitcast_fusion.5
  414.2 4.6 cosine_bitcast_fusion
  422.9 4.7 fusion.10
  429.0 5.4 collective-permute-done.3
  437.8 17.8 %collective-permute-done.5 = f32[2,2,1,256,256]{4,3,1,0,2:T(8,128)} collective-permute-done((f32[2,2,1,256,256]{4,3,1,0,2:T(8,128)}, f32[2,2,1,256,256]{4,3,1,0,2:T(8,128)}, u32[]{:S(2)}, u32[]{:S(2)}) %collective-permute-start.5) | collective-permute-done | bytes 1048608 | tf_op jit(solution)/shard_map/ppermute | solution.py:151
  455.6 4.3 maximum_bitcast_fusion.1
  459.9 5.0 gather_fusion.1
  464.9 5.3 copy.440
  470.1 4.6 fusion.639
  508.5 4.3 fusion.14
  514.8 19.2 %reduce-scatter.5.cloned.1.call-done = f32[256,256]{0,1:T(8,128)} async-done(((f32[256,1024]{0,1:T(8,128)}), f32[256,256]{0,1:T(8,128)}) %reduce-scatter.5.cloned.1.call-update) | async-done | bytes 262160 | tf_op jit(solution)/shard_map/reduce_scatter | solution.py:157
  (190 shorter events, 252.1 us)
Async XLA Ops:
  9.0 1.6 copy-start.19
  38.1 5.1 copy-start.22
  38.1 7.0 %copy-start.20 = (f32[1,256,1024]{2,1,0:T(8,128)S(1)}, f32[1,256,1024]{2,1,0:T(8,128)}, u32[]{:S(2)}) copy-start(f32[1,256,1024]{2,1,0:T(8,128)} %param.7) | copy-start | bytes 3145732
  38.1 53.8 %all-to-all-start = ((f32[2,2,1,256,1024]{3,0,2,1,4:T(2,128)}), f32[2,2,1,256,1024]{3,0,2,1,4:T(2,128)}, u32[]{:S(2)}, u32[]{:S(2)}) async-start(f32[2,2,1,256,1024]{3,0,2,1,4:T(2,128)} %copy.362), calls=%async_computation | async-start | bytes 8388608 | tf_op jit(solution)/shard_map/all_to_all | solution.py:141
  43.1 120.4 %all-reduce.3.cloned.1.call-start = ((), (), s32[]{:S(2)}) async-start(), calls=%async_computation.6 | async-start | bytes 4194304 | tf_op jit(solution)/shard_map/psum | solution.py:30
  51.8 78.8 %copy-start.8 = (f32[8,128,256]{2,1,0:T(8,128)}, f32[8,128,256]{2,1,0:T(8,128)S(1)}, u32[]{:S(2)}) copy-start(f32[8,128,256]{2,1,0:T(8,128)S(1)} %get-tuple-element.75) | copy-start | bytes 3145732
  159.6 24.0 %collective-permute-start = (f32[2,2,1,256,256]{4,3,1,0,2:T(8,128)}, f32[2,2,1,256,256]{4,3,1,0,2:T(8,128)}, u32[]{:S(2)}, u32[]{:S(2)}) collective-permute-start(f32[2,2,1,256,256]{4,3,1,0,2:T(8,128)} %bitcast.451), channel_id=1, source_target_pairs={{0,4},{4,8},{8,12},{12,0},{1,5},{5,9},{9,13},{13,1},{2,6},{6,10},{... | collective-permute-start | bytes 3145736 | tf_op jit(solution)/shard_map/ppermute | solution.py:151
  160.7 26.4 %collective-permute-start.1 = (f32[2,2,1,256,256]{4,3,1,0,2:T(8,128)}, f32[2,2,1,256,256]{4,3,1,0,2:T(8,128)}, u32[]{:S(2)}, u32[]{:S(2)}) collective-permute-start(f32[2,2,1,256,256]{4,3,1,0,2:T(8,128)} %bitcast.450), channel_id=1, source_target_pairs={{0,8},{4,12},{8,0},{12,4},{1,9},{5,13},{9,1},{13,5},{2,10},{6,14},... | collective-permute-start | bytes 3145736 | tf_op jit(solution)/shard_map/ppermute | solution.py:151
  161.7 43.4 %collective-permute-start.2 = (f32[2,2,1,256,256]{4,3,1,0,2:T(8,128)}, f32[2,2,1,256,256]{4,3,1,0,2:T(8,128)}, u32[]{:S(2)}, u32[]{:S(2)}) collective-permute-start(f32[2,2,1,256,256]{4,3,1,0,2:T(8,128)} %bitcast.449), channel_id=1, source_target_pairs={{0,12},{4,0},{8,4},{12,8},{1,13},{5,1},{9,5},{13,9},{2,14},{6,2},{... | collective-permute-start | bytes 3145736 | tf_op jit(solution)/shard_map/ppermute | solution.py:151
  168.3 2.9 copy-start.11
  168.3 2.9 copy-start.12
  226.4 3.2 copy-start.6
  231.9 1.9 copy-start.13
  233.7 2.0 copy-start.7
  247.7 1.3 copy-start.1
  249.0 1.5 copy-start.17
  264.1 3.6 copy-start.2
  264.1 3.6 copy-start.14
  267.7 2.0 copy-start.5
  289.6 53.2 %all-to-all-start.1 = ((f32[2,2,1,256,1024]{3,0,2,1,4:T(2,128)}), f32[2,2,1,256,1024]{3,0,2,1,4:T(2,128)}, u32[]{:S(2)}, u32[]{:S(2)}) async-start(f32[2,2,1,256,1024]{3,0,2,1,4:T(2,128)} %copy.413), calls=%async_computation.1 | async-start | bytes 8388608 | tf_op jit(solution)/shard_map/all_to_all | solution.py:141
  294.5 220.3 %reduce-scatter.3.cloned.1.call-start = ((), (), s32[]{:S(2)}) async-start(), calls=%async_computation.4 | async-start | bytes 1310720 | tf_op jit(solution)/shard_map/reduce_scatter | solution.py:157
  410.3 24.1 %collective-permute-start.3 = (f32[2,2,1,256,256]{4,3,1,0,2:T(8,128)}, f32[2,2,1,256,256]{4,3,1,0,2:T(8,128)}, u32[]{:S(2)}, u32[]{:S(2)}) collective-permute-start(f32[2,2,1,256,256]{4,3,1,0,2:T(8,128)} %bitcast.447), channel_id=1, source_target_pairs={{0,4},{4,8},{8,12},{12,0},{1,5},{5,9},{9,13},{13,1},{2,6},{6,10},{... | collective-permute-start | bytes 3145736 | tf_op jit(solution)/shard_map/ppermute | solution.py:151
  410.3 3.8 copy-start.21
  411.4 26.4 %collective-permute-start.4 = (f32[2,2,1,256,256]{4,3,1,0,2:T(8,128)}, f32[2,2,1,256,256]{4,3,1,0,2:T(8,128)}, u32[]{:S(2)}, u32[]{:S(2)}) collective-permute-start(f32[2,2,1,256,256]{4,3,1,0,2:T(8,128)} %bitcast.446), channel_id=1, source_target_pairs={{0,8},{4,12},{8,0},{12,4},{1,9},{5,13},{9,1},{13,5},{2,10},{6,14},... | collective-permute-start | bytes 3145736 | tf_op jit(solution)/shard_map/ppermute | solution.py:151
  412.7 42.9 %collective-permute-start.5 = (f32[2,2,1,256,256]{4,3,1,0,2:T(8,128)}, f32[2,2,1,256,256]{4,3,1,0,2:T(8,128)}, u32[]{:S(2)}, u32[]{:S(2)}) collective-permute-start(f32[2,2,1,256,256]{4,3,1,0,2:T(8,128)} %bitcast.445), channel_id=1, source_target_pairs={{0,12},{4,0},{8,4},{12,8},{1,13},{5,1},{9,5},{13,9},{2,14},{6,2},{... | collective-permute-start | bytes 3145736 | tf_op jit(solution)/shard_map/ppermute | solution.py:151
  427.5 1.3 copy-start.18
  428.8 105.1 %reduce-scatter.5.cloned.1.call-start = ((), (), s32[]{:S(2)}) async-start(), calls=%async_computation.5 | async-start | bytes 1310720 | tf_op jit(solution)/shard_map/reduce_scatter | solution.py:157
  476.9 3.2 copy-start.3
  482.3 1.9 copy-start.15
  484.2 2.0 copy-start.4
  495.8 2.3 copy-start.10
  498.1 2.5 copy-start
  (2 other events, 2.5 us)
Sparse Core Ops, SparseCore 0:
  46.9 90.1 all-reduce.2
  428.9 29.9 reduce-scatter.2
  502.7 31.1 reduce-scatter.4
